TPU v7x, 512 devices: a whole 4x4x16 slice. The times are simulated.
512 devices in a mesh: section: 8 (over y, z_hi), dp: 16 (over z_lo, core), chan: 4 (over x).
Axes of the slice: x: 4, y: 4, z: 16 (z_hi: 2, z_lo: 8; z = z_hi * 8 + z_lo), core: 2. Of those that a mesh axis runs over, the one named last changes fastest.
Arguments:
- clips: bfloat16 [2, 512, 2048], P(None, 'chan', 'dp'), may hold values from -6 to 6
- weights: bfloat16 [8, 512, 27, 512], P('section', ('chan', 'dp')), may hold values from -0.0546875 to 0.0546875
- cotangents: bfloat16 [2, 512, 2048], P(None, 'chan', 'dp'), may hold values from -0.5 to 0.5
Outputs:
- weight_grads: float32 [8, 512, 27, 512], P('section', ('chan', 'dp'))
All inputs are finite; a program needn't handle non-finite values.
Results may differ from a plain program's by a relative error of at most 0.019.
Values may be sent and summed in bfloat16 or wider, within the bound.
No kernel may reach another device: no remote copies, remote signals or barrier semaphores. Data moves between devices by JAX's collectives and lax.ppermute only.
A program may use at most 128 MiB of HBM per device.

v0:
```python
import jax
import jax.numpy as jnp
from jax import lax
from jax.sharding import PartitionSpec as P

FRAMES = 4
HEIGHT = 4
WIDTH = 8
MICRO = 2


def from_partner(block, axis, distance):
    count = lax.axis_size(axis)
    route = []
    for low in range(count):
        high = low | 1 << distance
        if high != low and high < count:
            route += [(low, high), (high, low)]
    return lax.ppermute(block, axis, route)


def with_halo(shard, sides, width):
    for axis, dim in sides:
        size, length = (lax.axis_size(axis), shard.shape[dim])
        up = [(i, (i + 1) % size) for i in range(size - 1)]
        down = [(j, i) for i, j in up]
        last = lax.slice_in_dim(shard, length - width, length, axis=dim)
        first = lax.slice_in_dim(shard, 0, width, axis=dim)
        before = lax.ppermute(last, axis, up)
        after = lax.ppermute(first, axis, down)
        shard = jnp.concatenate([before, shard, after], axis=dim)
    return shard


def as_sent(shard):

    def short(part):
        return part.astype(jnp.bfloat16) if part.dtype == jnp.float32 else part

    return jax.tree.map(short, shard)


def silu_slope(values):
    sigmoid = jax.nn.sigmoid(values)
    return sigmoid * (1.0 + values * (1.0 - sigmoid))


def shifted_taps(source, time_shift, mirror, frames, height, columns):
    cell_count = source.shape[1]
    plane_size = height * columns
    margin = plane_size + columns + 1
    padded = jnp.pad(source, ((0, 0), (margin, margin)))
    position = jnp.arange(cell_count, dtype=jnp.int32)
    frame_of = position // plane_size % frames
    row_of = position // columns % height
    column_of = position % columns
    windows = []
    for row_shift in range(3):
        for column_shift in range(3):
            if mirror:
                move_frame, move_row, move_column = (
                    1 - time_shift,
                    1 - row_shift,
                    1 - column_shift,
                )
            else:
                move_frame, move_row, move_column = (
                    time_shift - 1,
                    row_shift - 1,
                    column_shift - 1,
                )
            offset = move_frame * plane_size + move_row * columns + move_column
            window = padded[:, margin + offset : margin + offset + cell_count]
            inside = (
                (frame_of + move_frame >= 0)
                & (frame_of + move_frame < frames)
                & (row_of + move_row >= 0)
                & (row_of + move_row < height)
                & (column_of + move_column >= 0)
                & (column_of + move_column < columns)
            )
            windows.append(jnp.where(inside[None, :], window, jnp.zeros_like(window)))
    return windows


def arrange_kernel(kernel):
    outputs = kernel.shape[0]
    inputs = kernel.shape[2]
    return kernel.reshape(outputs, 3, 9 * inputs).transpose(1, 0, 2)


def conv_forward(activated, arranged, frames, height, columns):
    outputs = arranged.shape[1]
    result = jnp.zeros((outputs, activated.shape[1]), jnp.float32)
    for time_shift in range(3):
        stacked = jnp.concatenate(
            shifted_taps(activated, time_shift, False, frames, height, columns), axis=0
        )
        result = result + jnp.dot(arranged[time_shift], stacked, preferred_element_type=jnp.float32)
    return result


def conv_input_grad(grads_all, arranged, frames, height, columns):
    outputs = arranged.shape[1]
    inputs = arranged.shape[2] // 9
    cell_count = grads_all.shape[1]
    result = jnp.zeros((inputs, cell_count), jnp.float32)
    for time_shift in range(3):
        stacked = jnp.stack(
            shifted_taps(grads_all, time_shift, True, frames, height, columns), axis=1
        )
        stacked = stacked.reshape(-1, cell_count)
        matrix = arranged[time_shift].reshape(outputs * 9, inputs)
        result = result + lax.dot_general(
            matrix, stacked, (((0,), (0,)), ((), ())), preferred_element_type=jnp.float32
        )
    return result


def weight_grad_from_grads(activated, grad_low, frames, height, columns):
    outputs = grad_low.shape[0]
    cell_count = grad_low.shape[1]
    pieces = []
    for time_shift in range(3):
        stacked = jnp.stack(
            shifted_taps(grad_low, time_shift, True, frames, height, columns), axis=1
        )
        stacked = stacked.reshape(outputs * 9, cell_count)
        product = lax.dot_general(
            stacked, activated, (((1,), (1,)), ((), ())), preferred_element_type=jnp.float32
        )
        pieces.append(product.reshape(outputs, 9, activated.shape[0]))
    return jnp.concatenate(pieces, axis=1)


def mirror_pair(source):
    for bit_index in range(lax.axis_size("section").bit_length() - 1):
        source = from_partner(source, "section", bit_index)
    return source


def kernel_mirror(source):
    for bit_index in range(lax.axis_size("section").bit_length() - 1):
        source = from_partner(source, "section", bit_index)
    return source


def mirror_grads(source):
    for bit_index in range(lax.axis_size("section").bit_length() - 1):
        source = from_partner(source.astype(jnp.bfloat16), "section", bit_index).astype(
            source.dtype
        )
    return source


def channel_gather(source):
    return lax.all_gather(source, "chan", axis=0, tiled=True)


def section_rims(source):
    return with_halo(source[None], (("section", 0),), 1)


def active_lane(tick_index, positions, spacing, per_lane, lane_count):
    offsets = tick_index - positions
    first_aligned = offsets[0] % spacing == 0
    lane_now = jnp.where(first_aligned, 0, lane_count - 1).astype(jnp.int32)
    offset = jnp.where(first_aligned, offsets[0], offsets[lane_count - 1])
    slot_now = offset // spacing
    is_valid = (offset % spacing == 0) & (slot_now >= 0) & (slot_now < per_lane)
    return (lane_now, jnp.clip(slot_now, 0, per_lane - 1), is_valid)


def store_slot(buffer, lane_now, slot_now, is_valid, payload):
    chosen = jnp.where(is_valid, payload, buffer[lane_now, slot_now])
    starts = (lane_now, slot_now) + (0,) * payload.ndim
    return lax.dynamic_update_slice(buffer, chosen[None, None], starts)


def receive_slots(buffer, anchors, keep_mask, tick_index, spacing, per_lane, payload):
    for lane_index in range(anchors.shape[0]):
        offset = tick_index - anchors[lane_index]
        slot_now = offset // spacing
        is_valid = (
            keep_mask[lane_index]
            & (offset % spacing == 0)
            & (slot_now >= 0)
            & (slot_now < per_lane)
        )
        buffer = store_slot(
            buffer, lane_index, jnp.clip(slot_now, 0, per_lane - 1), is_valid, payload
        )
    return buffer


def branch_index(is_valid, lane_now):
    return jnp.where(is_valid, lane_now + 1, 0)


def on_device(clips, weights, cotangents):
    sections = lax.axis_size("section")
    section_id = lax.axis_index("section")
    half_depth = sections // 2
    local_rows = clips.shape[1]
    cell_count = clips.shape[2]
    channels = local_rows * lax.axis_size("chan")
    own_share = weights[0]
    lane_shares = jnp.stack([own_share, kernel_mirror(own_share)])
    lane_layers = jnp.stack([section_id, sections - 1 - section_id])
    lane_first = jnp.array([0, MICRO // 2], jnp.int32)
    per_lane = MICRO // 2
    spacing = 2
    lane_count = lane_shares.shape[0]
    lane_kernels = lax.all_gather(lane_shares, "dp", axis=1, tiled=True)
    arranged_lanes = [arrange_kernel(lane_kernels[lane_index]) for lane_index in range(lane_count)]
    tick_count = sections + spacing * (per_lane - 1)

    def forward_tick(tick_index, carried):
        incoming, inputs_buf, skip_buf, acts_buf = carried
        lane_now, slot_now, is_valid = active_lane(
            tick_index, lane_layers, spacing, per_lane, lane_count
        )
        layer_now = lane_layers[lane_now]
        clip_now = clips[lane_first[lane_now] + slot_now]
        state_now = jnp.where(layer_now == 0, clip_now, incoming[lane_now])
        skip_now = skip_buf[lane_now, slot_now]
        summed = state_now.astype(jnp.float32) + skip_now.astype(jnp.float32)
        activated = jax.nn.silu(summed).astype(jnp.bfloat16)
        acts_all = channel_gather(activated)

        def forward_skipped():
            return jnp.zeros(state_now.shape, jnp.float32)

        def forward_make_branch(lane_index):

            def convolve():
                return conv_forward(acts_all, arranged_lanes[lane_index], FRAMES, HEIGHT, WIDTH)

            return convolve

        branches = [forward_skipped] + [
            forward_make_branch(lane_index) for lane_index in range(lane_count)
        ]
        update = lax.switch(branch_index(is_valid, lane_now), branches)
        output = (state_now.astype(jnp.float32) + update).astype(jnp.bfloat16)
        inputs_buf = store_slot(inputs_buf, lane_now, slot_now, is_valid, state_now)
        acts_buf = store_slot(acts_buf, lane_now, slot_now, is_valid, acts_all)
        outgoing = jnp.where(is_valid & (layer_now < half_depth), output, jnp.zeros_like(output))
        arrived = mirror_pair(outgoing)
        skip_buf = receive_slots(
            skip_buf,
            sections - 1 - lane_layers,
            lane_layers >= half_depth,
            tick_index,
            spacing,
            per_lane,
            arrived,
        )
        rim_rows = section_rims(output)
        incoming = jnp.stack([rim_rows[0], rim_rows[2]])
        return (incoming, inputs_buf, skip_buf, acts_buf)

    empty_rows = jnp.zeros((lane_count, local_rows, cell_count), jnp.bfloat16)
    empty_slots = jnp.zeros((lane_count, per_lane, local_rows, cell_count), jnp.bfloat16)
    empty_acts = jnp.zeros((lane_count, per_lane, channels, cell_count), jnp.bfloat16)
    forward_out = lax.fori_loop(
        0, tick_count, forward_tick, (empty_rows, empty_slots, empty_slots, empty_acts)
    )
    inputs_buf, skip_buf, acts_buf = (forward_out[1], forward_out[2], forward_out[3])

    def backward_tick(tick_index, carried):
        incoming, gskip_buf, glow_buf = carried
        lane_now, slot_now, is_valid = active_lane(
            tick_index, sections - 1 - lane_layers, spacing, per_lane, lane_count
        )
        layer_now = lane_layers[lane_now]
        cotangent_now = cotangents[lane_first[lane_now] + slot_now]
        upstream = jnp.where(layer_now == sections - 1, cotangent_now, incoming[lane_now]).astype(
            jnp.float32
        )
        upstream = upstream + gskip_buf[lane_now, slot_now].astype(jnp.float32)
        grad_low = upstream.astype(jnp.bfloat16)
        summed = inputs_buf[lane_now, slot_now].astype(jnp.float32) + skip_buf[
            lane_now, slot_now
        ].astype(jnp.float32)

        def backward_skipped():
            return jnp.zeros((channels, cell_count), jnp.float32)

        def backward_make_branch(lane_index):

            def differentiate():
                return conv_input_grad(grad_low, arranged_lanes[lane_index], FRAMES, HEIGHT, WIDTH)

            return differentiate

        branches = [backward_skipped] + [
            backward_make_branch(lane_index) for lane_index in range(lane_count)
        ]
        partial_terms = lax.switch(branch_index(is_valid, lane_now), branches)
        pre_grad = jax.tree.map(
            lambda part: part.astype(jnp.float32),
            lax.psum_scatter(as_sent(partial_terms), "chan", scatter_dimension=0, tiled=True),
        ) * silu_slope(summed)
        glow_buf = store_slot(glow_buf, lane_now, slot_now, is_valid, grad_low)
        sent = (upstream + pre_grad).astype(jnp.bfloat16)
        skip_low = pre_grad.astype(jnp.bfloat16)
        outgoing = jnp.where(
            is_valid & (layer_now >= half_depth), skip_low, jnp.zeros_like(skip_low)
        )
        arrived = mirror_pair(outgoing)
        gskip_buf = receive_slots(
            gskip_buf, lane_layers, lane_layers < half_depth, tick_index, spacing, per_lane, arrived
        )
        rim_rows = section_rims(sent)
        incoming = jnp.stack([rim_rows[2], rim_rows[0]])
        return (incoming, gskip_buf, glow_buf)

    backward_out = lax.fori_loop(
        0, tick_count, backward_tick, (empty_rows, empty_slots, empty_slots)
    )
    glow_buf = backward_out[2]
    grads_rows = lax.all_to_all(glow_buf, "dp", split_axis=2, concat_axis=3, tiled=True)
    acts_cells = lax.all_gather(acts_buf, "dp", axis=3, tiled=True)
    lane_grads = []
    for lane_index in range(lane_count):
        total = weight_grad_from_grads(
            acts_cells[lane_index, 0], grads_rows[lane_index, 0], FRAMES, HEIGHT, WIDTH
        )
        lane_grads.append(total)
    own_grads = lane_grads[0] + mirror_grads(lane_grads[1])
    return own_grads[None]


def solution(mesh):
    placed = (
        P(None, "chan", "dp"),
        P("section", ("chan", "dp"), None, None),
        P(None, "chan", "dp"),
    )
    return jax.shard_map(
        on_device,
        mesh=mesh,
        in_specs=placed,
        out_specs=P("section", ("chan", "dp"), None, None),
        check_vma=False,
    )
```

profile of v0, /device:TPU:8, one launch (start us, length us, event | category | flops | bytes accessed | tf_op | source)
XLA Modules:
  0.0 1673.4 jit_solution(5137266346502927320)
XLA Ops:
  6.5 15.7 collective-permute-start.10
  62.8 129.0 %all-gather.3.cloned.1.call-done = bf16[2,128,27,512]{3,0,2,1:T(2,128)(2,1)} async-done(((bf16[2,8,27,512]{3,0,2,1:T(2,128)(2,1)}), bf16[2,128,27,512]{3,0,2,1:T(2,128)(2,1)}) %all-gather.3.cloned.1.call-update) | async-done | bytes 7077904 | tf_op jit(solution)/shard_map/all_gather | solution.py:214
  191.8 15.5 fusion.311
  207.2 14.8 copy.1660
  226.2 14.8 copy.1661
  245.3 529.0 %while.42 = (s32[]{:T(128)}, bf16[2,128,128]{1,2,0:T(8,128)(2,1)S(1)}, bf16[2,1,128,128]{2,3,1,0:T(8,128)(2,1)S(1)}, bf16[2,1,128,128]{2,3,1,0:T(8,128)(2,1)S(1)...) while((s32[]{:T(128)}, ...), condition=%wide.region_4.5_spmd, body=%wide.region_0.4_spmd.sunk | while | flops 455368896 | bytes 31049684 | solution.py:266
  543.1 13.5 collective-permute-start.2
  775.6 744.8 %while.43 = (s32[]{:T(128)}, bf16[2,128,128]{1,2,0:T(8,128)(2,1)S(1)}, bf16[2,1,128,128]{2,3,1,0:T(8,128)(2,1)}, bf16[2,1,128,128]{2,3,1,0:T(8,128)(2,1)}, s32[2...) while((s32[]{:T(128)}, ...), condition=%wide.region_10.11_spmd, body=%wide.region_5.10_spmd.sunk | while | flops 454528576 | bytes 34589428 | solution.py:319
  787.0 36.6 %reduce-scatter.6.cloned.1.call-done = bf16[128,128]{1,0:T(8,128)(2,1)} async-done(((bf16[512,128]{1,0:T(8,128)(2,1)}), bf16[128,128]{1,0:T(8,128)(2,1)}) %reduce-scatter.6.cloned.1.call-update) | async-done | bytes 32784 | tf_op jit(solution)/shard_map/while
  881.8 35.2 %reduce-scatter.6.cloned.1.call-done = bf16[128,128]{1,0:T(8,128)(2,1)} async-done(((bf16[512,128]{1,0:T(8,128)(2,1)}), bf16[128,128]{1,0:T(8,128)(2,1)}) %reduce-scatter.6.cloned.1.call-update) | async-done | bytes 32784 | tf_op jit(solution)/shard_map/while
  934.2 13.5 collective-permute-start.6
  973.5 17.4 %conditional.5 = (bf16[512,128]{0,1:T(8,128)(2,1)S(1)}) conditional(s32[]{:T(128)} %clamp.25, () %tuple.419, (bf16[128,128]{0,1:T(8,128)(2,1)S(1)}, bf16[3,128,4608]{2,1,0:T(8,128)(2,1)}) %tuple.420, (bf16[128,128]{0,1:T(8,128)(2,1)S(1)}, bf16[3,128,4608]{2,1,0:T(8,128)(2,1)}) %tuple.421), branch_computations={%region_6.6_spmd, %region_7.7_spmd, %region_8.8_spmd} | conditional | flops 453791232 | bytes 30786196 | solution.py:300
  992.4 17.1 %reduce-scatter.6.cloned.1.call-done = bf16[128,128]{1,0:T(8,128)(2,1)} async-done(((bf16[512,128]{1,0:T(8,128)(2,1)}), bf16[128,128]{1,0:T(8,128)(2,1)}) %reduce-scatter.6.cloned.1.call-update) | async-done | bytes 32784 | tf_op jit(solution)/shard_map/while
  1026.8 13.5 collective-permute-start.6
  1067.6 35.2 %reduce-scatter.6.cloned.1.call-done = bf16[128,128]{1,0:T(8,128)(2,1)} async-done(((bf16[512,128]{1,0:T(8,128)(2,1)}), bf16[128,128]{1,0:T(8,128)(2,1)}) %reduce-scatter.6.cloned.1.call-update) | async-done | bytes 32784 | tf_op jit(solution)/shard_map/while
  1120.2 13.5 collective-permute-start.6
  1161.0 35.2 %reduce-scatter.6.cloned.1.call-done = bf16[128,128]{1,0:T(8,128)(2,1)} async-done(((bf16[512,128]{1,0:T(8,128)(2,1)}), bf16[128,128]{1,0:T(8,128)(2,1)}) %reduce-scatter.6.cloned.1.call-update) | async-done | bytes 32784 | tf_op jit(solution)/shard_map/while
  1213.5 13.5 collective-permute-start.6
  1252.8 17.4 %conditional.5 = (bf16[512,128]{0,1:T(8,128)(2,1)S(1)}) conditional(s32[]{:T(128)} %clamp.25, () %tuple.419, (bf16[128,128]{0,1:T(8,128)(2,1)S(1)}, bf16[3,128,4608]{2,1,0:T(8,128)(2,1)}) %tuple.420, (bf16[128,128]{0,1:T(8,128)(2,1)S(1)}, bf16[3,128,4608]{2,1,0:T(8,128)(2,1)}) %tuple.421), branch_computations={%region_6.6_spmd, %region_7.7_spmd, %region_8.8_spmd} | conditional | flops 453791232 | bytes 30786196 | solution.py:300
  1271.7 17.0 %reduce-scatter.6.cloned.1.call-done = bf16[128,128]{1,0:T(8,128)(2,1)} async-done(((bf16[512,128]{1,0:T(8,128)(2,1)}), bf16[128,128]{1,0:T(8,128)(2,1)}) %reduce-scatter.6.cloned.1.call-update) | async-done | bytes 32784 | tf_op jit(solution)/shard_map/while
  1306.1 13.5 collective-permute-start.6
  1346.9 35.2 %reduce-scatter.6.cloned.1.call-done = bf16[128,128]{1,0:T(8,128)(2,1)} async-done(((bf16[512,128]{1,0:T(8,128)(2,1)}), bf16[128,128]{1,0:T(8,128)(2,1)}) %reduce-scatter.6.cloned.1.call-update) | async-done | bytes 32784 | tf_op jit(solution)/shard_map/while
  1440.2 33.5 %reduce-scatter.6.cloned.1.call-done = bf16[128,128]{1,0:T(8,128)(2,1)} async-done(((bf16[512,128]{1,0:T(8,128)(2,1)}), bf16[128,128]{1,0:T(8,128)(2,1)}) %reduce-scatter.6.cloned.1.call-update) | async-done | bytes 32784 | tf_op jit(solution)/shard_map/while
  1557.2 66.0 %all-gather.5.cloned.1.call-done = bf16[2,1,512,2048]{2,3,1,0:T(8,128)(2,1)} async-done(((bf16[2,1,512,128]{2,3,1,0:T(8,128)(2,1)}), bf16[2,1,512,2048]{2,3,1,0:T(8,128)(2,1)}) %all-gather.5.cloned.1.call-update) | async-done | bytes 4194320 | tf_op jit(solution)/shard_map/all_gather | solution.py:324
  (946 shorter events, 963.1 us)
Async XLA Ops:
  6.5 185.2 %all-gather.3.cloned.1.call-start = ((), (), s32[]{:S(2)}) async-start(), calls=%async_computation.2 | async-start | bytes 7520256 | tf_op jit(solution)/shard_map/all_gather | solution.py:214
  264.8 42.8 %collective-permute-start = (bf16[1,128,128]{1,2,0:T(8,128)(2,1)S(1)}, bf16[1,128,128]{1,2,0:T(8,128)(2,1)S(1)}, u32[]{:S(2)}, u32[]{:S(2)}) collective-permute-start(bf16[1,128,128]{1,2,0:T(8,128)(2,1)S(1)} %fusion.351), channel_id=1, source_target_pairs={{64,0},{128,64},{192,128},{256,192},{320,256},{384,320},{448,384},... | collective-permute-start | bytes 98312 | tf_op jit(solution)/shard_map/while/body/eval_jaxpr/ppermute | solution.py:30
  272.2 35.5 %collective-permute-start.1 = (bf16[1,128,128]{1,2,0:T(8,128)(2,1)S(1)}, bf16[1,128,128]{1,2,0:T(8,128)(2,1)S(1)}, u32[]{:S(2)}, u32[]{:S(2)}) collective-permute-start(bf16[1,128,128]{1,2,0:T(8,128)(2,1)S(1)} %fusion.351), channel_id=1, source_target_pairs={{0,64},{64,128},{128,192},{192,256},{256,320},{320,384},{384,448},... | collective-permute-start | bytes 98312 | tf_op jit(solution)/shard_map/while/body/eval_jaxpr/ppermute | solution.py:29
  331.7 42.8 %collective-permute-start = (bf16[1,128,128]{1,2,0:T(8,128)(2,1)S(1)}, bf16[1,128,128]{1,2,0:T(8,128)(2,1)S(1)}, u32[]{:S(2)}, u32[]{:S(2)}) collective-permute-start(bf16[1,128,128]{1,2,0:T(8,128)(2,1)S(1)} %fusion.351), channel_id=1, source_target_pairs={{64,0},{128,64},{192,128},{256,192},{320,256},{384,320},{448,384},... | collective-permute-start | bytes 98312 | tf_op jit(solution)/shard_map/while/body/eval_jaxpr/ppermute | solution.py:30
  340.9 33.7 %collective-permute-start.1 = (bf16[1,128,128]{1,2,0:T(8,128)(2,1)S(1)}, bf16[1,128,128]{1,2,0:T(8,128)(2,1)S(1)}, u32[]{:S(2)}, u32[]{:S(2)}) collective-permute-start(bf16[1,128,128]{1,2,0:T(8,128)(2,1)S(1)} %fusion.351), channel_id=1, source_target_pairs={{0,64},{64,128},{128,192},{192,256},{256,320},{320,384},{384,448},... | collective-permute-start | bytes 98312 | tf_op jit(solution)/shard_map/while/body/eval_jaxpr/ppermute | solution.py:29
  400.5 37.5 %collective-permute-start = (bf16[1,128,128]{1,2,0:T(8,128)(2,1)S(1)}, bf16[1,128,128]{1,2,0:T(8,128)(2,1)S(1)}, u32[]{:S(2)}, u32[]{:S(2)}) collective-permute-start(bf16[1,128,128]{1,2,0:T(8,128)(2,1)S(1)} %fusion.351), channel_id=1, source_target_pairs={{64,0},{128,64},{192,128},{256,192},{320,256},{384,320},{448,384},... | collective-permute-start | bytes 98312 | tf_op jit(solution)/shard_map/while/body/eval_jaxpr/ppermute | solution.py:30
  403.4 34.6 %collective-permute-start.1 = (bf16[1,128,128]{1,2,0:T(8,128)(2,1)S(1)}, bf16[1,128,128]{1,2,0:T(8,128)(2,1)S(1)}, u32[]{:S(2)}, u32[]{:S(2)}) collective-permute-start(bf16[1,128,128]{1,2,0:T(8,128)(2,1)S(1)} %fusion.351), channel_id=1, source_target_pairs={{0,64},{64,128},{128,192},{192,256},{256,320},{320,384},{384,448},... | collective-permute-start | bytes 98312 | tf_op jit(solution)/shard_map/while/body/eval_jaxpr/ppermute | solution.py:29
  462.0 43.3 %collective-permute-start = (bf16[1,128,128]{1,2,0:T(8,128)(2,1)S(1)}, bf16[1,128,128]{1,2,0:T(8,128)(2,1)S(1)}, u32[]{:S(2)}, u32[]{:S(2)}) collective-permute-start(bf16[1,128,128]{1,2,0:T(8,128)(2,1)S(1)} %fusion.351), channel_id=1, source_target_pairs={{64,0},{128,64},{192,128},{256,192},{320,256},{384,320},{448,384},... | collective-permute-start | bytes 98312 | tf_op jit(solution)/shard_map/while/body/eval_jaxpr/ppermute | solution.py:30
  467.7 37.6 %collective-permute-start.1 = (bf16[1,128,128]{1,2,0:T(8,128)(2,1)S(1)}, bf16[1,128,128]{1,2,0:T(8,128)(2,1)S(1)}, u32[]{:S(2)}, u32[]{:S(2)}) collective-permute-start(bf16[1,128,128]{1,2,0:T(8,128)(2,1)S(1)} %fusion.351), channel_id=1, source_target_pairs={{0,64},{64,128},{128,192},{192,256},{256,320},{320,384},{384,448},... | collective-permute-start | bytes 98312 | tf_op jit(solution)/shard_map/while/body/eval_jaxpr/ppermute | solution.py:29
  525.9 46.7 %collective-permute-start = (bf16[1,128,128]{1,2,0:T(8,128)(2,1)S(1)}, bf16[1,128,128]{1,2,0:T(8,128)(2,1)S(1)}, u32[]{:S(2)}, u32[]{:S(2)}) collective-permute-start(bf16[1,128,128]{1,2,0:T(8,128)(2,1)S(1)} %fusion.351), channel_id=1, source_target_pairs={{64,0},{128,64},{192,128},{256,192},{320,256},{384,320},{448,384},... | collective-permute-start | bytes 98312 | tf_op jit(solution)/shard_map/while/body/eval_jaxpr/ppermute | solution.py:30
  536.1 36.6 %collective-permute-start.1 = (bf16[1,128,128]{1,2,0:T(8,128)(2,1)S(1)}, bf16[1,128,128]{1,2,0:T(8,128)(2,1)S(1)}, u32[]{:S(2)}, u32[]{:S(2)}) collective-permute-start(bf16[1,128,128]{1,2,0:T(8,128)(2,1)S(1)} %fusion.351), channel_id=1, source_target_pairs={{0,64},{64,128},{128,192},{192,256},{256,320},{320,384},{384,448},... | collective-permute-start | bytes 98312 | tf_op jit(solution)/shard_map/while/body/eval_jaxpr/ppermute | solution.py:29
  598.4 37.5 %collective-permute-start = (bf16[1,128,128]{1,2,0:T(8,128)(2,1)S(1)}, bf16[1,128,128]{1,2,0:T(8,128)(2,1)S(1)}, u32[]{:S(2)}, u32[]{:S(2)}) collective-permute-start(bf16[1,128,128]{1,2,0:T(8,128)(2,1)S(1)} %fusion.351), channel_id=1, source_target_pairs={{64,0},{128,64},{192,128},{256,192},{320,256},{384,320},{448,384},... | collective-permute-start | bytes 98312 | tf_op jit(solution)/shard_map/while/body/eval_jaxpr/ppermute | solution.py:30
  660.4 43.2 %collective-permute-start = (bf16[1,128,128]{1,2,0:T(8,128)(2,1)S(1)}, bf16[1,128,128]{1,2,0:T(8,128)(2,1)S(1)}, u32[]{:S(2)}, u32[]{:S(2)}) collective-permute-start(bf16[1,128,128]{1,2,0:T(8,128)(2,1)S(1)} %fusion.351), channel_id=1, source_target_pairs={{64,0},{128,64},{192,128},{256,192},{320,256},{384,320},{448,384},... | collective-permute-start | bytes 98312 | tf_op jit(solution)/shard_map/while/body/eval_jaxpr/ppermute | solution.py:30
  724.0 44.8 %collective-permute-start = (bf16[1,128,128]{1,2,0:T(8,128)(2,1)S(1)}, bf16[1,128,128]{1,2,0:T(8,128)(2,1)S(1)}, u32[]{:S(2)}, u32[]{:S(2)}) collective-permute-start(bf16[1,128,128]{1,2,0:T(8,128)(2,1)S(1)} %fusion.351), channel_id=1, source_target_pairs={{64,0},{128,64},{192,128},{256,192},{320,256},{384,320},{448,384},... | collective-permute-start | bytes 98312 | tf_op jit(solution)/shard_map/while/body/eval_jaxpr/ppermute | solution.py:30
  736.4 32.4 %collective-permute-start.1 = (bf16[1,128,128]{1,2,0:T(8,128)(2,1)S(1)}, bf16[1,128,128]{1,2,0:T(8,128)(2,1)S(1)}, u32[]{:S(2)}, u32[]{:S(2)}) collective-permute-start(bf16[1,128,128]{1,2,0:T(8,128)(2,1)S(1)} %fusion.351), channel_id=1, source_target_pairs={{0,64},{64,128},{128,192},{192,256},{256,320},{320,384},{384,448},... | collective-permute-start | bytes 98312 | tf_op jit(solution)/shard_map/while/body/eval_jaxpr/ppermute | solution.py:29
  775.6 48.0 %reduce-scatter.6.cloned.1.call-start = ((), (), s32[]{:S(2)}) async-start(), calls=%async_computation.4 | async-start | bytes 163840 | tf_op jit(solution)/shard_map/while
  870.3 46.6 %reduce-scatter.6.cloned.1.call-start = ((), (), s32[]{:S(2)}) async-start(), calls=%async_computation.4 | async-start | bytes 163840 | tf_op jit(solution)/shard_map/while
  963.6 45.8 %reduce-scatter.6.cloned.1.call-start = ((), (), s32[]{:S(2)}) async-start(), calls=%async_computation.4 | async-start | bytes 163840 | tf_op jit(solution)/shard_map/while
  1056.2 46.7 %reduce-scatter.6.cloned.1.call-start = ((), (), s32[]{:S(2)}) async-start(), calls=%async_computation.4 | async-start | bytes 163840 | tf_op jit(solution)/shard_map/while
  1149.6 46.6 %reduce-scatter.6.cloned.1.call-start = ((), (), s32[]{:S(2)}) async-start(), calls=%async_computation.4 | async-start | bytes 163840 | tf_op jit(solution)/shard_map/while
  1243.0 45.8 %reduce-scatter.6.cloned.1.call-start = ((), (), s32[]{:S(2)}) async-start(), calls=%async_computation.4 | async-start | bytes 163840 | tf_op jit(solution)/shard_map/while
  1335.5 46.6 %reduce-scatter.6.cloned.1.call-start = ((), (), s32[]{:S(2)}) async-start(), calls=%async_computation.4 | async-start | bytes 163840 | tf_op jit(solution)/shard_map/while
  1428.8 44.9 %reduce-scatter.6.cloned.1.call-start = ((), (), s32[]{:S(2)}) async-start(), calls=%async_computation.4 | async-start | bytes 163840 | tf_op jit(solution)/shard_map/while
  1520.4 102.8 %all-gather.5.cloned.1.call-start = ((), (), s32[]{:S(2)}) async-start(), calls=%async_computation.3 | async-start | bytes 4456448 | tf_op jit(solution)/shard_map/all_gather | solution.py:324
  (127 other events, 2578.9 us)
Sparse Core Ops, SparseCore 0:
  62.8 128.8 all-gather.2
  786.4 37.1 reduce-scatter.5
  881.2 35.7 reduce-scatter.5
  991.8 17.6 reduce-scatter.5
  1067.1 35.7 reduce-scatter.5
  1160.4 35.7 reduce-scatter.5
  1271.2 17.5 reduce-scatter.5
  1346.3 35.7 reduce-scatter.5
  1439.6 33.9 reduce-scatter.5
  1523.0 100.1 all-gather.4
where the time goes:
time: 1680 us; the launch traced here: 1670 us
  waiting for transfers between devices  607 us (36%)
  starting transfers between devices  570 us (34%)
  local copies, waits for them, and re-layouts  177 us (11%)
  loops' own time  125 us (7%)
  blocking collectives  86.9 us (5%)
  other arithmetic  74.3 us (4%)
  matrix products  19 us (1%)
    ppermute x54, starting transfers between devices, from_partner(): return lax.ppermute(block, axis, route)  323 us
    while x16, waiting for transfers between devices  245 us
    ppermute x16, starting transfers between devices, with_halo(): after = lax.ppermute(first, axis, down)  175 us
    ppermute x54, waiting for transfers between devices, from_partner(): return lax.ppermute(block, axis, route)  156 us
    all_gather x1, waiting for transfers between devices, on_device(): lane_kernels = lax.all_gather(lane_shares, 'dp', axis=1, tiled=True)  129 us
    all_gather x8, blocking collectives, channel_gather(): return lax.all_gather(source, 'chan', axis=0, tiled=True)  86.9 us
    ppermute x16, starting transfers between devices, with_halo(): before = lax.ppermute(last, axis, up)  67.9 us
    another operation x1, loops' own time, on_device(): lax.fori_loop(0, tick_count, forward_tick, (empty_rows, empty_slots, empt...  67.6 us
  transfers between devices with their start and end apart: 97, of which 52 were waited for; matrix products, arithmetic and copies ran while one was open for 3% of the time, Pallas kernels for 0%

commit v1 on v0

--- a/solution.py
+++ b/solution.py
@@ -7,6 +7,13 @@
 HEIGHT = 4
 WIDTH = 8
 MICRO = 2
+
+
+def gather_over(array, axis, d):
+    size = lax.axis_size(axis)
+    tiles = jnp.stack([array for _ in range(size)])
+    tiles = lax.all_to_all(tiles, axis, split_axis=0, concat_axis=0)
+    return jnp.concatenate(tiles, axis=d)
 
 
 def from_partner(block, axis, distance):
@@ -154,7 +161,7 @@
 
 
 def channel_gather(source):
-    return lax.all_gather(source, "chan", axis=0, tiled=True)
+    return gather_over(source, "chan", 0)
 
 
 def section_rims(source):

time: 1680 us -> 1610 us (0.958)
  blocking collectives: 86.9 us -> 0 us
  starting transfers between devices: 570 us -> 593 us
  waiting for transfers between devices: 607 us -> 590 us
    all_gather x8 -> x0, blocking collectives: 86.9 us -> none  [channel_gather(): return lax.all_gather(source, 'chan', axis=0, tiled=True)]
    all_to_all x0 -> x8, starting transfers between devices: none -> 27.6 us  [gather_over(): tiles = lax.all_to_all(tiles, axis, split_axis=0, concat_axis=0)]
    ppermute x54, waiting for transfers between devices: 156 us -> 130 us  [from_partner(): return lax.ppermute(block, axis, route)]
  transfers between devices with their start and end apart: 97 -> 105, of which waited for: 52 -> 58; matrix products, arithmetic and copies ran while one was open for 3% -> 3% of each run, Pallas kernels for 0% -> 0%
where the time goes in v1:
time: 1610 us; the launch traced here: 1600 us
  starting transfers between devices  593 us (37%)
  waiting for transfers between devices  590 us (37%)
  local copies, waits for them, and re-layouts  182 us (11%)
  loops' own time  119 us (7%)
  other arithmetic  79.6 us (5%)
  matrix products  21.4 us (1%)
    ppermute x54, starting transfers between devices, from_partner(): return lax.ppermute(block, axis, route)  317 us
    while x16, waiting for transfers between devices  252 us
    ppermute x16, starting transfers between devices, with_halo(): after = lax.ppermute(first, axis, down)  178 us
    ppermute x54, waiting for transfers between devices, from_partner(): return lax.ppermute(block, axis, route)  130 us
    all_gather x1, waiting for transfers between devices, on_device(): lane_kernels = lax.all_gather(lane_shares, 'dp', axis=1, tiled=True)  129 us
    ppermute x16, starting transfers between devices, with_halo(): before = lax.ppermute(last, axis, up)  66.9 us
    another operation x1, loops' own time, on_device(): lax.fori_loop(0, tick_count, forward_tick, (empty_rows, empty_slots, empt...  65.8 us
    another operation x1, loops' own time, on_device(): lax.fori_loop(0, tick_count, backward_tick, (empty_rows, empty_slots, emp...  51.5 us
  transfers between devices with their start and end apart: 105, of which 58 were waited for; matrix products, arithmetic and copies ran while one was open for 3% of the time, Pallas kernels for 0%

profile of v1, /device:TPU:8, one launch (start us, length us, event | category | flops | bytes accessed | tf_op | source)
XLA Modules:
  0.0 1599.1 jit_solution(17969269928388429419)
XLA Ops:
  6.5 15.7 collective-permute-start.10
  62.8 129.0 %all-gather.3.cloned.1.call-done = bf16[2,128,27,512]{3,0,2,1:T(2,128)(2,1)} async-done(((bf16[2,8,27,512]{3,0,2,1:T(2,128)(2,1)}), bf16[2,128,27,512]{3,0,2,1:T(2,128)(2,1)}) %all-gather.3.cloned.1.call-update) | async-done | bytes 7077904 | tf_op jit(solution)/shard_map/all_gather | solution.py:221
  191.8 15.4 fusion.313
  207.2 14.8 copy.1589
  226.2 14.8 copy.1590
  245.3 455.0 %while.42 = (s32[]{:T(128)}, bf16[2,128,128]{1,2,0:T(8,128)(2,1)S(1)}, bf16[2,1,128,128]{2,3,1,0:T(8,128)(2,1)S(1)}, bf16[2,1,128,128]{2,3,1,0:T(8,128)(2,1)S(1)...) while((s32[]{:T(128)}, ...), condition=%wide.region_4.5_spmd, body=%wide.region_0.4_spmd.sunk | while | flops 455368896 | bytes 30984176 | solution.py:273
  431.8 18.7 %collective-permute-start.2 = (bf16[128,128]{0,1:T(8,128)(2,1)S(1)}, bf16[128,128]{0,1:T(8,128)(2,1)S(1)}, u32[]{:S(2)}, u32[]{:S(2)}) collective-permute-start(bf16[128,128]{0,1:T(8,128)(2,1)S(1)} %broadcast_select_fusion.4), channel_id=1, source_target_pairs={{0,64},{64,0},{128,192},{192,128},{256,320},{320,256},{384,448},{4... | collective-permute-start | bytes 98312 | tf_op jit(solution)/shard_map/while/body/eval_jaxpr/ppermute | solution.py:26
  667.6 17.3 %collective-permute-start = (bf16[1,128,128]{1,2,0:T(8,128)(2,1)S(1)}, bf16[1,128,128]{1,2,0:T(8,128)(2,1)S(1)}, u32[]{:S(2)}, u32[]{:S(2)}) collective-permute-start(bf16[1,128,128]{1,2,0:T(8,128)(2,1)S(1)} %fusion.355), channel_id=1, source_target_pairs={{64,0},{128,64},{192,128},{256,192},{320,256},{384,320},{448,384},... | collective-permute-start | bytes 98312 | tf_op jit(solution)/shard_map/while/body/eval_jaxpr/ppermute | solution.py:37
  702.3 748.0 %while.43 = (s32[]{:T(128)}, bf16[2,128,128]{1,2,0:T(8,128)(2,1)}, bf16[2,1,128,128]{2,3,1,0:T(8,128)(2,1)}, bf16[2,1,128,128]{2,3,1,0:T(8,128)(2,1)}, s32[2]{0:...) while((s32[]{:T(128)}, bf16[2,128,128]{1,2,0:T(8,128)(2,1)}, ...), condition=%wide.region_10.11_spmd, body=%wide.region_5.10_spmd.sunk | while | flops 454528576 | bytes 34589428 | solution.py:326
  713.4 41.7 %reduce-scatter.6.cloned.1.call-done = bf16[128,128]{1,0:T(8,128)(2,1)} async-done(((bf16[512,128]{1,0:T(8,128)(2,1)}), bf16[128,128]{1,0:T(8,128)(2,1)}) %reduce-scatter.6.cloned.1.call-update) | async-done | bytes 32784 | tf_op jit(solution)/shard_map/while
  772.4 13.5 collective-permute-start.6
  812.8 35.2 %reduce-scatter.6.cloned.1.call-done = bf16[128,128]{1,0:T(8,128)(2,1)} async-done(((bf16[512,128]{1,0:T(8,128)(2,1)}), bf16[128,128]{1,0:T(8,128)(2,1)}) %reduce-scatter.6.cloned.1.call-update) | async-done | bytes 32784 | tf_op jit(solution)/shard_map/while
  865.3 13.5 collective-permute-start.6
  904.2 17.4 %conditional.5 = (bf16[512,128]{0,1:T(8,128)(2,1)S(1)}) conditional(s32[]{:T(128)} %clamp.25, () %tuple.351, (bf16[128,128]{0,1:T(8,128)(2,1)S(1)}, bf16[3,128,4608]{2,1,0:T(8,128)(2,1)}) %tuple.352, (bf16[128,128]{0,1:T(8,128)(2,1)S(1)}, bf16[3,128,4608]{2,1,0:T(8,128)(2,1)}) %tuple.353), branch_computations={%region_6.6_spmd, %region_7.7_spmd, %region_8.8_spmd} | conditional | flops 453791232 | bytes 30786196 | solution.py:307
  923.0 17.7 %reduce-scatter.6.cloned.1.call-done = bf16[128,128]{1,0:T(8,128)(2,1)} async-done(((bf16[512,128]{1,0:T(8,128)(2,1)}), bf16[128,128]{1,0:T(8,128)(2,1)}) %reduce-scatter.6.cloned.1.call-update) | async-done | bytes 32784 | tf_op jit(solution)/shard_map/while
  958.1 13.5 collective-permute-start.6
  998.4 35.2 %reduce-scatter.6.cloned.1.call-done = bf16[128,128]{1,0:T(8,128)(2,1)} async-done(((bf16[512,128]{1,0:T(8,128)(2,1)}), bf16[128,128]{1,0:T(8,128)(2,1)}) %reduce-scatter.6.cloned.1.call-update) | async-done | bytes 32784 | tf_op jit(solution)/shard_map/while
  1091.3 35.2 %reduce-scatter.6.cloned.1.call-done = bf16[128,128]{1,0:T(8,128)(2,1)} async-done(((bf16[512,128]{1,0:T(8,128)(2,1)}), bf16[128,128]{1,0:T(8,128)(2,1)}) %reduce-scatter.6.cloned.1.call-update) | async-done | bytes 32784 | tf_op jit(solution)/shard_map/while
  1182.8 17.4 %conditional.5 = (bf16[512,128]{0,1:T(8,128)(2,1)S(1)}) conditional(s32[]{:T(128)} %clamp.25, () %tuple.351, (bf16[128,128]{0,1:T(8,128)(2,1)S(1)}, bf16[3,128,4608]{2,1,0:T(8,128)(2,1)}) %tuple.352, (bf16[128,128]{0,1:T(8,128)(2,1)S(1)}, bf16[3,128,4608]{2,1,0:T(8,128)(2,1)}) %tuple.353), branch_computations={%region_6.6_spmd, %region_7.7_spmd, %region_8.8_spmd} | conditional | flops 453791232 | bytes 30786196 | solution.py:307
  1201.6 17.7 %reduce-scatter.6.cloned.1.call-done = bf16[128,128]{1,0:T(8,128)(2,1)} async-done(((bf16[512,128]{1,0:T(8,128)(2,1)}), bf16[128,128]{1,0:T(8,128)(2,1)}) %reduce-scatter.6.cloned.1.call-update) | async-done | bytes 32784 | tf_op jit(solution)/shard_map/while
  1276.9 35.4 %reduce-scatter.6.cloned.1.call-done = bf16[128,128]{1,0:T(8,128)(2,1)} async-done(((bf16[512,128]{1,0:T(8,128)(2,1)}), bf16[128,128]{1,0:T(8,128)(2,1)}) %reduce-scatter.6.cloned.1.call-update) | async-done | bytes 32784 | tf_op jit(solution)/shard_map/while
  1369.9 33.7 %reduce-scatter.6.cloned.1.call-done = bf16[128,128]{1,0:T(8,128)(2,1)} async-done(((bf16[512,128]{1,0:T(8,128)(2,1)}), bf16[128,128]{1,0:T(8,128)(2,1)}) %reduce-scatter.6.cloned.1.call-update) | async-done | bytes 32784 | tf_op jit(solution)/shard_map/while
  1487.3 50.0 %all-gather.5.cloned.1.call-done = bf16[2,1,512,2048]{3,2,1,0:T(8,128)(2,1)} async-done(((bf16[2,1,512,128]{3,2,1,0:T(8,128)(2,1)}), bf16[2,1,512,2048]{3,2,1,0:T(8,128)(2,1)}) %all-gather.5.cloned.1.call-update) | async-done | bytes 4194320 | tf_op jit(solution)/shard_map/all_gather | solution.py:331
  1554.1 16.1 %collective-permute-done.13 = bf16[8,27,512]{2,1,0:T(8,128)(2,1)S(1)} collective-permute-done((bf16[8,27,512]{2,1,0:T(8,128)(2,1)S(1)}, bf16[8,27,512]{2,1,0:T(8,128)(2,1)S(1)}, u32[]{:S(2)}, u32[]{:S(2)}) %collective-permute-start.13) | collective-permute-done | bytes 221216 | tf_op jit(solution)/shard_map/ppermute | solution.py:26
  (960 shorter events, 892.5 us)
Async XLA Ops:
  6.5 185.2 %all-gather.3.cloned.1.call-start = ((), (), s32[]{:S(2)}) async-start(), calls=%async_computation.3 | async-start | bytes 7520256 | tf_op jit(solution)/shard_map/all_gather | solution.py:221
  271.4 29.7 %collective-permute-start = (bf16[1,128,128]{1,2,0:T(8,128)(2,1)S(1)}, bf16[1,128,128]{1,2,0:T(8,128)(2,1)S(1)}, u32[]{:S(2)}, u32[]{:S(2)}) collective-permute-start(bf16[1,128,128]{1,2,0:T(8,128)(2,1)S(1)} %fusion.355), channel_id=1, source_target_pairs={{64,0},{128,64},{192,128},{256,192},{320,256},{384,320},{448,384},... | collective-permute-start | bytes 98312 | tf_op jit(solution)/shard_map/while/body/eval_jaxpr/ppermute | solution.py:37
  328.9 27.5 %collective-permute-start = (bf16[1,128,128]{1,2,0:T(8,128)(2,1)S(1)}, bf16[1,128,128]{1,2,0:T(8,128)(2,1)S(1)}, u32[]{:S(2)}, u32[]{:S(2)}) collective-permute-start(bf16[1,128,128]{1,2,0:T(8,128)(2,1)S(1)} %fusion.355), channel_id=1, source_target_pairs={{64,0},{128,64},{192,128},{256,192},{320,256},{384,320},{448,384},... | collective-permute-start | bytes 98312 | tf_op jit(solution)/shard_map/while/body/eval_jaxpr/ppermute | solution.py:37
  431.8 33.3 %collective-permute-start.2 = (bf16[128,128]{0,1:T(8,128)(2,1)S(1)}, bf16[128,128]{0,1:T(8,128)(2,1)S(1)}, u32[]{:S(2)}, u32[]{:S(2)}) collective-permute-start(bf16[128,128]{0,1:T(8,128)(2,1)S(1)} %broadcast_select_fusion.4), channel_id=1, source_target_pairs={{0,64},{64,0},{128,192},{192,128},{256,320},{320,256},{384,448},{4... | collective-permute-start | bytes 98312 | tf_op jit(solution)/shard_map/while/body/eval_jaxpr/ppermute | solution.py:26
  556.6 30.1 %collective-permute-start = (bf16[1,128,128]{1,2,0:T(8,128)(2,1)S(1)}, bf16[1,128,128]{1,2,0:T(8,128)(2,1)S(1)}, u32[]{:S(2)}, u32[]{:S(2)}) collective-permute-start(bf16[1,128,128]{1,2,0:T(8,128)(2,1)S(1)} %fusion.355), channel_id=1, source_target_pairs={{64,0},{128,64},{192,128},{256,192},{320,256},{384,320},{448,384},... | collective-permute-start | bytes 98312 | tf_op jit(solution)/shard_map/while/body/eval_jaxpr/ppermute | solution.py:37
  667.6 30.4 %collective-permute-start = (bf16[1,128,128]{1,2,0:T(8,128)(2,1)S(1)}, bf16[1,128,128]{1,2,0:T(8,128)(2,1)S(1)}, u32[]{:S(2)}, u32[]{:S(2)}) collective-permute-start(bf16[1,128,128]{1,2,0:T(8,128)(2,1)S(1)} %fusion.355), channel_id=1, source_target_pairs={{64,0},{128,64},{192,128},{256,192},{320,256},{384,320},{448,384},... | collective-permute-start | bytes 98312 | tf_op jit(solution)/shard_map/while/body/eval_jaxpr/ppermute | solution.py:37
  702.5 52.6 %reduce-scatter.6.cloned.1.call-start = ((), (), s32[]{:S(2)}) async-start(), calls=%async_computation.5 | async-start | bytes 163840 | tf_op jit(solution)/shard_map/while
  756.8 29.2 %collective-permute-start.7 = (bf16[128,128]{0,1:T(8,128)(2,1)S(1)}, bf16[128,128]{0,1:T(8,128)(2,1)S(1)}, u32[]{:S(2)}, u32[]{:S(2)}) collective-permute-start(bf16[128,128]{0,1:T(8,128)(2,1)S(1)} %convert_select_fusion.2), channel_id=1, source_target_pairs={{0,64},{64,0},{128,192},{192,128},{256,320},{320,256},{384,448},{4... | collective-permute-start | bytes 98312 | tf_op jit(solution)/shard_map/while/body/eval_jaxpr/ppermute | solution.py:26
  801.8 46.2 %reduce-scatter.6.cloned.1.call-start = ((), (), s32[]{:S(2)}) async-start(), calls=%async_computation.5 | async-start | bytes 163840 | tf_op jit(solution)/shard_map/while
  849.7 29.2 %collective-permute-start.7 = (bf16[128,128]{0,1:T(8,128)(2,1)S(1)}, bf16[128,128]{0,1:T(8,128)(2,1)S(1)}, u32[]{:S(2)}, u32[]{:S(2)}) collective-permute-start(bf16[128,128]{0,1:T(8,128)(2,1)S(1)} %convert_select_fusion.2), channel_id=1, source_target_pairs={{0,64},{64,0},{128,192},{192,128},{256,320},{320,256},{384,448},{4... | collective-permute-start | bytes 98312 | tf_op jit(solution)/shard_map/while/body/eval_jaxpr/ppermute | solution.py:26
  894.7 46.0 %reduce-scatter.6.cloned.1.call-start = ((), (), s32[]{:S(2)}) async-start(), calls=%async_computation.5 | async-start | bytes 163840 | tf_op jit(solution)/shard_map/while
  942.4 29.2 %collective-permute-start.7 = (bf16[128,128]{0,1:T(8,128)(2,1)S(1)}, bf16[128,128]{0,1:T(8,128)(2,1)S(1)}, u32[]{:S(2)}, u32[]{:S(2)}) collective-permute-start(bf16[128,128]{0,1:T(8,128)(2,1)S(1)} %convert_select_fusion.2), channel_id=1, source_target_pairs={{0,64},{64,0},{128,192},{192,128},{256,320},{320,256},{384,448},{4... | collective-permute-start | bytes 98312 | tf_op jit(solution)/shard_map/while/body/eval_jaxpr/ppermute | solution.py:26
  987.5 46.2 %reduce-scatter.6.cloned.1.call-start = ((), (), s32[]{:S(2)}) async-start(), calls=%async_computation.5 | async-start | bytes 163840 | tf_op jit(solution)/shard_map/while
  1035.4 29.2 %collective-permute-start.7 = (bf16[128,128]{0,1:T(8,128)(2,1)S(1)}, bf16[128,128]{0,1:T(8,128)(2,1)S(1)}, u32[]{:S(2)}, u32[]{:S(2)}) collective-permute-start(bf16[128,128]{0,1:T(8,128)(2,1)S(1)} %convert_select_fusion.2), channel_id=1, source_target_pairs={{0,64},{64,0},{128,192},{192,128},{256,320},{320,256},{384,448},{4... | collective-permute-start | bytes 98312 | tf_op jit(solution)/shard_map/while/body/eval_jaxpr/ppermute | solution.py:26
  1080.4 46.2 %reduce-scatter.6.cloned.1.call-start = ((), (), s32[]{:S(2)}) async-start(), calls=%async_computation.5 | async-start | bytes 163840 | tf_op jit(solution)/shard_map/while
  1128.3 29.2 %collective-permute-start.7 = (bf16[128,128]{0,1:T(8,128)(2,1)S(1)}, bf16[128,128]{0,1:T(8,128)(2,1)S(1)}, u32[]{:S(2)}, u32[]{:S(2)}) collective-permute-start(bf16[128,128]{0,1:T(8,128)(2,1)S(1)} %convert_select_fusion.2), channel_id=1, source_target_pairs={{0,64},{64,0},{128,192},{192,128},{256,320},{320,256},{384,448},{4... | collective-permute-start | bytes 98312 | tf_op jit(solution)/shard_map/while/body/eval_jaxpr/ppermute | solution.py:26
  1173.3 45.9 %reduce-scatter.6.cloned.1.call-start = ((), (), s32[]{:S(2)}) async-start(), calls=%async_computation.5 | async-start | bytes 163840 | tf_op jit(solution)/shard_map/while
  1221.0 29.2 %collective-permute-start.7 = (bf16[128,128]{0,1:T(8,128)(2,1)S(1)}, bf16[128,128]{0,1:T(8,128)(2,1)S(1)}, u32[]{:S(2)}, u32[]{:S(2)}) collective-permute-start(bf16[128,128]{0,1:T(8,128)(2,1)S(1)} %convert_select_fusion.2), channel_id=1, source_target_pairs={{0,64},{64,0},{128,192},{192,128},{256,320},{320,256},{384,448},{4... | collective-permute-start | bytes 98312 | tf_op jit(solution)/shard_map/while/body/eval_jaxpr/ppermute | solution.py:26
  1266.0 46.3 %reduce-scatter.6.cloned.1.call-start = ((), (), s32[]{:S(2)}) async-start(), calls=%async_computation.5 | async-start | bytes 163840 | tf_op jit(solution)/shard_map/while
  1314.0 29.2 %collective-permute-start.7 = (bf16[128,128]{0,1:T(8,128)(2,1)S(1)}, bf16[128,128]{0,1:T(8,128)(2,1)S(1)}, u32[]{:S(2)}, u32[]{:S(2)}) collective-permute-start(bf16[128,128]{0,1:T(8,128)(2,1)S(1)} %convert_select_fusion.2), channel_id=1, source_target_pairs={{0,64},{64,0},{128,192},{192,128},{256,320},{320,256},{384,448},{4... | collective-permute-start | bytes 98312 | tf_op jit(solution)/shard_map/while/body/eval_jaxpr/ppermute | solution.py:26
  1359.0 44.6 %reduce-scatter.6.cloned.1.call-start = ((), (), s32[]{:S(2)}) async-start(), calls=%async_computation.5 | async-start | bytes 163840 | tf_op jit(solution)/shard_map/while
  1405.3 29.1 %collective-permute-start.7 = (bf16[128,128]{0,1:T(8,128)(2,1)S(1)}, bf16[128,128]{0,1:T(8,128)(2,1)S(1)}, u32[]{:S(2)}, u32[]{:S(2)}) collective-permute-start(bf16[128,128]{0,1:T(8,128)(2,1)S(1)} %convert_select_fusion.2), channel_id=1, source_target_pairs={{0,64},{64,0},{128,192},{192,128},{256,320},{320,256},{384,448},{4... | collective-permute-start | bytes 98312 | tf_op jit(solution)/shard_map/while/body/eval_jaxpr/ppermute | solution.py:26
  1450.3 87.0 %all-gather.5.cloned.1.call-start = ((), (), s32[]{:S(2)}) async-start(), calls=%async_computation.4 | async-start | bytes 4456448 | tf_op jit(solution)/shard_map/all_gather | solution.py:331
  1543.3 26.9 %collective-permute-start.13 = (bf16[8,27,512]{2,1,0:T(8,128)(2,1)S(1)}, bf16[8,27,512]{2,1,0:T(8,128)(2,1)S(1)}, u32[]{:S(2)}, u32[]{:S(2)}) collective-permute-start(bf16[8,27,512]{2,1,0:T(8,128)(2,1)S(1)} %pad_maximum_fusion.3), channel_id=1, source_target_pairs={{0,64},{64,0},{128,192},{192,128},{256,320},{320,256},{384,448},{4... | collective-permute-start | bytes 663560 | tf_op jit(solution)/shard_map/ppermute | solution.py:26
  (135 other events, 2616.7 us)
Sparse Core Ops, SparseCore 0:
  62.8 128.8 all-gather.2
  712.9 42.1 reduce-scatter.5
  812.2 35.7 reduce-scatter.5
  922.5 18.2 reduce-scatter.5
  997.9 35.7 reduce-scatter.5
  1090.8 35.7 reduce-scatter.5
  1201.1 18.1 reduce-scatter.5
  1276.4 35.8 reduce-scatter.5
  1369.4 34.1 reduce-scatter.5
  1452.8 84.4 all-gather.4
